TPU v7x, 256 devices: a whole 4x4x8 slice. The times are simulated.
256 devices in a mesh: side: 2 (over y_hi), row: 8 (over z), col: 16 (over x, y_lo, core).
Axes of the slice: x: 4, y: 4 (y_hi: 2, y_lo: 2; y = y_hi * 2 + y_lo), z: 8, core: 2. Of those that a mesh axis runs over, the one named last changes fastest.
Arguments:
- queries: bfloat16 [512, 8192], P(('row', 'col')), may hold values from -4.5 to 16
- new_entries: bfloat16 [512, 2048], P(('row', 'col')), may hold values from -4.5 to 15.875
- cache_keys: bfloat16 [2, 512, 256, 1024], P('side', ('row', 'col')), may hold values from -4.5 to 16
- cache_values: bfloat16 [2, 512, 256, 1024], P('side', ('row', 'col')), may hold values from -6 to 6
- lengths: int32 [512], P(('row', 'col')), may hold values from 1 to 256, 32768 in all
- residual: bfloat16 [512, 8192], P(None, 'col'), may hold values from -16 to 16
- norm_gain: bfloat16 [8192], P('col'), may hold values from 0.099609375 to 1.8984375
- out_weight: bfloat16 [2, 8192, 8192], P('side', 'row', 'col'), may hold values from -0.125 to 0.125
- gate_weight: bfloat16 [2, 8192, 14336], P('side', 'col', 'row'), may hold values from -0.0625 to 0.0625
- up_weight: bfloat16 [2, 8192, 14336], P('side', 'col', 'row'), may hold values from -0.0625 to 0.0625
- down_weight: bfloat16 [2, 14336, 8192], P('side', 'row', 'col'), may hold values from -0.046875 to 0.046875
Outputs:
- layer_out: bfloat16 [512, 8192], P(('row', 'col'), 'side')
All inputs are finite; a program needn't handle non-finite values. No bound on the sum of `lengths` on one device may be relied on, other than what follows from the above.
Results may differ from a plain program's by a relative error of at most 0.025.
Values may be sent and summed in bfloat16 or wider, within the bound.
No kernel may reach another device: no remote copies, remote signals or barrier semaphores. Data moves between devices by JAX's collectives and lax.ppermute only.
A program may use at most 64 MiB of HBM per device.

v0:
```python
import jax
import jax.numpy as jnp
from jax import lax
from jax.sharding import PartitionSpec as P

D = 8192
H = 64
KVH = 8
HD = 128
ORIG = 64
rope_theta = 500000.0
stretch_factor = 8.0
eps = 1e-05


def from_behind(value, axis, steps):
    count = lax.axis_size(axis)
    first, last = (max(0, -steps), min(count, count - steps))
    return lax.ppermute(value, axis, [(source, source + steps) for source in range(first, last)])


def frequencies(lengths):
    seq = lengths.astype(jnp.float32) + 1.0
    stretch = jnp.maximum(stretch_factor * seq / ORIG - (stretch_factor - 1.0), 1.0)
    log_base = jnp.log(jnp.float32(rope_theta)) + HD / (HD - 2.0) * jnp.log(stretch)
    expo = jnp.arange(HD // 2).astype(jnp.float32) * (2.0 / HD)
    return jnp.exp(-expo[None, :] * log_base[:, None])


def rotary(vec, angles):
    half = vec.shape[-1] // 2
    first = vec[..., :half]
    second = vec[..., half:]
    cosine = jnp.cos(angles)
    sine = jnp.sin(angles)
    return jnp.concatenate(
        [first * cosine - second * sine, second * cosine + first * sine], axis=-1
    )


def attention(queries, new_entries, keys, values, lengths):
    slots = queries.shape[0]
    span = keys.shape[1]
    per_group = H // KVH
    freqs = frequencies(lengths)
    angle_new = lengths.astype(jnp.float32)[:, None] * freqs
    angle_cache = jnp.arange(span).astype(jnp.float32)[None, :, None] * freqs[:, None, :]
    query_rot = rotary(
        queries.astype(jnp.float32).reshape(slots, H, HD), angle_new[:, None, :]
    ).astype(jnp.bfloat16)
    query_rot = query_rot.reshape(slots, KVH, per_group, HD)
    key_fresh = new_entries[:, : KVH * HD].astype(jnp.float32).reshape(slots, KVH, HD)
    value_fresh = new_entries[:, KVH * HD :].astype(jnp.float32).reshape(slots, KVH, HD)
    key_new_rot = rotary(key_fresh, angle_new[:, None, :]).astype(jnp.bfloat16)
    key_rot = rotary(
        keys.astype(jnp.float32).reshape(slots, span, KVH, HD), angle_cache[:, :, None, :]
    ).astype(jnp.bfloat16)
    scale = HD ** (-0.5)
    scores = (
        jnp.einsum("sgqd,scgd->sgqc", query_rot, key_rot, preferred_element_type=jnp.float32)
        * scale
    )
    own_score = (
        jnp.einsum("sgqd,sgd->sgq", query_rot, key_new_rot, preferred_element_type=jnp.float32)
        * scale
    )
    valid_mask = (jnp.arange(span)[None, :] < lengths[:, None])[:, None, None, :]
    highest = jnp.maximum(jnp.max(jnp.where(valid_mask, scores, -1e30), axis=-1), own_score)
    weights = jnp.where(valid_mask, jnp.exp(scores - highest[..., None]), 0.0)
    own_weight = jnp.exp(own_score - highest)
    totals = jnp.sum(weights, axis=-1) + own_weight
    weights16 = weights.astype(jnp.bfloat16)
    mixed = jnp.einsum(
        "sgqc,scgd->sgqd",
        weights16,
        values.reshape(slots, span, KVH, HD),
        preferred_element_type=jnp.float32,
    )
    mixed = mixed + own_weight[..., None] * value_fresh[:, :, None, :]
    return (mixed / totals[..., None]).reshape(slots, H * HD).astype(jnp.bfloat16)


def local(
    queries,
    new_entries,
    cache_keys,
    cache_values,
    lengths,
    residual,
    norm_gain,
    out_weight,
    gate_weight,
    up_weight,
    down_weight,
):
    attended = attention(queries, new_entries, cache_keys[0], cache_values[0], lengths)
    slot_count = attended.shape[0]
    row_count = lax.axis_size("row")
    col_count = lax.axis_size("col")
    head_block = attended.shape[1] // row_count
    split_heads = attended.reshape(slot_count, row_count, head_block)
    moved = from_behind(split_heads, "side", 1)
    blocks = lax.all_to_all(moved, "row", split_axis=1, concat_axis=0, tiled=True)
    sectioned = blocks.reshape(row_count, 1, slot_count, head_block)
    out_block = out_weight[0]
    partial_value = jnp.einsum(
        "akjd,de->akje",
        lax.all_gather(sectioned, "col", axis=1, tiled=True),
        out_block,
        preferred_element_type=jnp.float32,
    )
    col_width = out_block.shape[1]
    total_rows = row_count * col_count * slot_count
    projected = lax.psum(
        partial_value.reshape(total_rows, col_width).astype(jnp.bfloat16), "row"
    ).astype(jnp.float32)
    stream = residual.astype(jnp.float32) + projected
    squares = lax.psum(jnp.sum(stream * stream, axis=1), "col")
    inv_rms = lax.rsqrt(squares / D + eps)
    normed = (stream * inv_rms[:, None] * norm_gain.astype(jnp.float32)[None, :]).astype(
        jnp.bfloat16
    )
    gate_block = gate_weight[0]
    up_block = up_weight[0]
    down_block = down_weight[0]
    gate_part = jnp.dot(normed, gate_block, preferred_element_type=jnp.float32)
    up_part = jnp.dot(normed, up_block, preferred_element_type=jnp.float32)
    gate_total, up_total = (
        lax.psum(gate_part.astype(jnp.bfloat16), "col").astype(jnp.float32),
        lax.psum(up_part.astype(jnp.bfloat16), "col").astype(jnp.float32),
    )
    hidden = (jax.nn.silu(gate_total) * up_total).astype(jnp.bfloat16)
    down_part = jnp.dot(hidden, down_block, preferred_element_type=jnp.float32)
    down_total = lax.psum(down_part.astype(jnp.bfloat16), "row").astype(jnp.float32)
    final = (stream + down_total).astype(jnp.bfloat16)
    group_rows = col_count * slot_count
    mine_rows = lax.dynamic_slice_in_dim(final, lax.axis_index("row") * group_rows, group_rows, 0)
    slot_rows = lax.all_to_all(mine_rows, "col", split_axis=0, concat_axis=1, tiled=True)
    half_width = slot_rows.shape[1] // 2
    returned = from_behind(slot_rows[:, :half_width], "side", -1)
    return jnp.where(lax.axis_index("side") == 0, returned, slot_rows[:, half_width:])


def solution(mesh):
    in_specs = (
        P(("row", "col"), None),
        P(("row", "col"), None),
        P("side", ("row", "col"), None, None),
        P("side", ("row", "col"), None, None),
        P(("row", "col")),
        P(None, "col"),
        P("col"),
        P("side", "row", "col"),
        P("side", "col", "row"),
        P("side", "col", "row"),
        P("side", "row", "col"),
    )
    out_specs = P(("row", "col"), "side")
    return jax.shard_map(local, mesh=mesh, in_specs=in_specs, out_specs=out_specs, check_vma=False)
```

profile of v0, /device:TPU:1, one launch (start us, length us, event | category | flops | bytes accessed | tf_op | source)
XLA Modules:
  0.0 439.4 jit_solution(3323142169381161737)
XLA Ops:
  6.5 0.8 convert_element_type.82
  7.3 0.7 multiply_add_fusion
  8.0 0.7 iota_compare_fusion
  8.7 3.9 copy.23
  12.7 4.2 fusion.50
  16.8 3.8 copy.32
  20.6 3.8 copy.33
  24.9 1.9 multiply_cosine_fusion
  27.1 4.7 %subtract_convert_fusion = (bf16[4,256,8,64]{3,1,2,0:T(8,128)(2,1)S(1)}, bf16[4,256,8,64]{3,1,2,0:T(8,128)(2,1)S(1)}) fusion(f32[4,256,8,64]{3,1,2,0:T(8,128)} %copy.33, f32[4,256,8,64]{3,1,2,0:T(8,128)} %copy.32, f32[4,256,64]{2,1,0:T(8,128)S(1)} %get-tuple-element.22, f32[4,256,64]{2,1,0:T(8,128)S(1)} %get-tuple-element.21), kind=kLoop, calls=%fused_computation.3 | loop fusion | flops 4194304 | bytes 6815744 | tf_op jit(solution)/shard_map/convert.6
  31.8 1.3 select_reduce_fusion
  33.4 0.6 copy.36
  34.0 0.4 fusion.30
  34.6 5.7 %collective-permute-start = (bf16[4,8,1024]{2,0,1:T(4,128)(2,1)S(1)}, bf16[4,8,1024]{2,0,1:T(4,128)(2,1)S(1)}, u32[]{:S(2)}, u32[]{:S(2)}) collective-permute-start(bf16[4,8,1024]{2,0,1:T(4,128)(2,1)S(1)} %copy.27), channel_id=1, source_target_pairs={{0,128},{1,129},{2,130},{3,131},{4,132},{5,133},{6,134},{7,135},{8... | collective-permute-start | bytes 196616 | tf_op jit(solution)/shard_map/ppermute | solution.py:19
  40.3 1.3 collective-permute-done
  41.6 15.3 %all_to_all.34 = bf16[4,8,1024]{2,0,1:T(4,128)(2,1)S(1)} all-to-all(bf16[4,8,1024]{2,0,1:T(4,128)(2,1)S(1)} %collective-permute-done), channel_id=1, replica_groups=mesh['side'=2,'row'=8,'col'=16] {'row'}, dimensions={1} | all-to-all | bytes 131072 | tf_op jit(solution)/shard_map/all_to_all | solution.py:103
  56.9 0.6 copy.28
  57.6 34.6 %all-gather.3.cloned.1.call-done = bf16[8,64,1,1024]{3,0,2,1:T(8,128)(2,1)} async-done(((bf16[8,4,1,1024]{3,0,2,1:T(8,128)(2,1)}), bf16[8,64,1,1024]{3,0,2,1:T(8,128)(2,1)}) %all-gather.3.cloned.1.call-update) | async-done | bytes 1048592 | tf_op jit(solution)/shard_map/all_gather | solution.py:108
  92.2 1.8 copy.29
  94.1 2.8 convolution_convert_fusion.2
  96.9 68.6 %all-reduce.5.cloned.1.call-done = bf16[512,512]{1,0:T(8,128)(2,1)} async-done(((bf16[512,512]{1,0:T(8,128)(2,1)}), bf16[512,512]{1,0:T(8,128)(2,1)}) %all-reduce.5.cloned.1.call-update) | async-done | bytes 524304 | tf_op jit(solution)/shard_map/psum | solution.py:114
  165.5 1.3 multiply_reduce_fusion
  166.8 31.7 %psum.36 = f32[512]{0:T(512)S(1)} all-reduce(f32[512]{0:T(512)S(1)} %get-tuple-element.13), channel_id=1, replica_groups=mesh['side'=2,'row'=8,'col'=16] {'col'}, use_global_device_ids=true, to_apply=%region_4.5 | all-reduce | flops 512 | bytes 4096 | tf_op jit(solution)/shard_map/psum | solution.py:118
  198.6 3.6 convolution_convert_fusion.1
  202.2 2.5 convolution_convert_fusion
  204.8 129.6 %all-reduce.9.cloned.1.call-done = (bf16[512,1792]{1,0:T(8,128)(2,1)}, bf16[512,1792]{1,0:T(8,128)(2,1)}) async-done(((bf16[512,1792]{1,0:T(8,128)(2,1)}, bf16[512,1792]{1,0:T(8,128)(2,1)}), (bf16[512,1792]{1,0:T(8,128)(2,1)}, bf16[512,1792]{1,0:T(8,128)(2,1)})) %all-reduce.9.cloned.1.call-update) | async-done | bytes 3670032 | tf_op jit(solution)/shard_map/psum | solution.py:130
  334.4 4.6 %fusion.16 = bf16[512,512]{1,0:T(8,128)(2,1)} fusion(bf16[1,1792,512]{2,1,0:T(8,128)(2,1)} %param.21, bf16[512,1792]{1,0:T(8,128)(2,1)} %get-tuple-element.5, bf16[512,1792]{1,0:T(8,128)(2,1)} %get-tuple-element.6), kind=kOutput, calls=%fused_computation.21 | convolution fusion | flops 947126272 | bytes 6029312 | tf_op jit(solution)/shard_map/dot_general | solution.py:133
  339.0 70.0 %all-reduce.7.cloned.1.call-done = bf16[512,512]{1,0:T(8,128)(2,1)} async-done(((bf16[512,512]{1,0:T(8,128)(2,1)}), bf16[512,512]{1,0:T(8,128)(2,1)}) %all-reduce.7.cloned.1.call-update) | async-done | bytes 524304 | tf_op jit(solution)/shard_map/psum | solution.py:134
  409.1 0.9 fusion.37
  409.9 16.1 %all_to_all.35 = bf16[16,4,512]{2,1,0:T(4,128)(2,1)S(1)} all-to-all(bf16[16,4,512]{2,1,0:T(4,128)(2,1)S(1)} %all_to_all.28), channel_id=1, replica_groups=mesh['side'=2,'row'=8,'col'=16] {'col'}, dimensions={0} | all-to-all | bytes 131072 | tf_op jit(solution)/shard_map/all_to_all | solution.py:138
  426.0 1.3 collective-permute-start.1
  427.3 4.9 %collective-permute-done.1 = bf16[4,4096]{1,0:T(4,128)(2,1)S(1)} collective-permute-done((bf16[4,4096]{1,0:T(4,128)(2,1)S(1)}, bf16[4,4096]{1,0:T(4,128)(2,1)S(1)}, u32[]{:S(2)}, u32[]{:S(2)}) %collective-permute-start.1) | collective-permute-done | bytes 32800 | tf_op jit(solution)/shard_map/ppermute | solution.py:19
  432.2 0.6 slice_select_fusion
  (44 shorter events, 1.2 us)
Async XLA Ops:
  6.5 192.0 %copy-start = (bf16[1,512,1792]{2,1,0:T(8,128)(2,1)S(1)}, bf16[1,512,1792]{2,1,0:T(8,128)(2,1)}, u32[]{:S(2)}) copy-start(bf16[1,512,1792]{2,1,0:T(8,128)(2,1)} %param.19) | copy-start | bytes 5505028
  6.5 85.7 %all-gather.3.cloned.1.call-start = ((), (), s32[]{:S(2)}) async-start(), calls=%async_computation.4 | async-start | bytes 1114112 | tf_op jit(solution)/shard_map/all_gather | solution.py:108
  20.6 3.8 copy-start.4
  20.6 3.9 copy-start.5
  31.8 1.6 copy-start.1
  34.6 7.0 %collective-permute-start = (bf16[4,8,1024]{2,0,1:T(4,128)(2,1)S(1)}, bf16[4,8,1024]{2,0,1:T(4,128)(2,1)S(1)}, u32[]{:S(2)}, u32[]{:S(2)}) collective-permute-start(bf16[4,8,1024]{2,0,1:T(4,128)(2,1)S(1)} %copy.27), channel_id=1, source_target_pairs={{0,128},{1,129},{2,130},{3,131},{4,132},{5,133},{6,134},{7,135},{8... | collective-permute-start | bytes 196616 | tf_op jit(solution)/shard_map/ppermute | solution.py:19
  57.5 108.0 %all-reduce.5.cloned.1.call-start = ((), (), s32[]{:S(2)}) async-start(), calls=%async_computation.2 | async-start | bytes 1048576 | tf_op jit(solution)/shard_map/psum | solution.py:114
  94.0 2.9 copy-start.6
  94.0 71.5 %copy-start.2 = (bf16[512,512]{1,0:T(8,128)(2,1)S(1)}, bf16[512,512]{1,0:T(8,128)(2,1)}, u32[]{:S(2)}) copy-start(bf16[512,512]{1,0:T(8,128)(2,1)} %param.16) | copy-start | bytes 1572868
  96.9 237.5 %all-reduce.9.cloned.1.call-start = ((), (), s32[]{:S(2)}) async-start(), calls=%async_computation.5 | async-start | bytes 7340032 | tf_op jit(solution)/shard_map/psum | solution.py:130
  198.6 3.7 copy-start.3
  198.6 3.7 copy-start.7
  204.7 204.3 %all-reduce.7.cloned.1.call-start = ((), (), s32[]{:S(2)}) async-start(), calls=%async_computation.3 | async-start | bytes 1048576 | tf_op jit(solution)/shard_map/psum | solution.py:134
  426.0 6.2 %collective-permute-start.1 = (bf16[4,4096]{1,0:T(4,128)(2,1)S(1)}, bf16[4,4096]{1,0:T(4,128)(2,1)S(1)}, u32[]{:S(2)}, u32[]{:S(2)}) collective-permute-start(bf16[4,4096]{1,0:T(4,128)(2,1)S(1)} %slice.46), channel_id=1, source_target_pairs={{128,0},{129,1},{130,2},{131,3},{132,4},{133,5},{134,6},{135,7},{1... | collective-permute-start | bytes 98312 | tf_op jit(solution)/shard_map/ppermute | solution.py:19
Sparse Core Ops, SparseCore 0:
  57.7 34.5 all-gather.2
  97.0 68.4 all-reduce.4
  204.8 129.5 all-reduce.8
  339.1 69.8 all-reduce.6
where the time goes:
time: 440 us; the launch traced here: 439 us
  waiting for transfers between devices  309 us (70%)
  blocking collectives  63.1 us (14%)
  local copies, waits for them, and re-layouts  19 us (4%)
  matrix products  15.5 us (4%)
  between operations  13.3 us (3%)
  other arithmetic  12.2 us (3%)
  starting transfers between devices  7.07 us (2%)
    psum x1, waiting for transfers between devices, local(): lax.psum(up_part.astype(jnp.bfloat16), 'col').astype(jnp.float32)  130 us
    psum x1, waiting for transfers between devices, local(): lax.psum(down_part.astype(jnp.bfloat16), 'row').astype(jnp.float32)  70 us
    psum x1, waiting for transfers between devices, local(): lax.psum(partial_value.reshape(total_rows, col_width).astype(jnp.bfloat16...  68.6 us
    all_gather x1, waiting for transfers between devices, local(): lax.all_gather(sectioned, 'col', axis=1, tiled=True)  34.6 us
    psum x1, blocking collectives, local(): squares = lax.psum(jnp.sum(stream * stream, axis=1), 'col')  31.7 us
    all_to_all x1, blocking collectives, local(): lax.all_to_all(mine_rows, 'col', split_axis=0, concat_axis=1, tiled=True)  16.1 us
    all_to_all x1, blocking collectives, local(): lax.all_to_all(moved, 'row', split_axis=1, concat_axis=0, tiled=True)  15.3 us
    unnamed x21, local copies, waits for them, and re-layouts  12.2 us
  transfers between devices with their start and end apart: 6, of which 6 were waited for; matrix products, arithmetic and copies ran while one was open for 0% of the time, Pallas kernels for 0%

commit v1 on v0

--- a/solution.py
+++ b/solution.py
@@ -1,3 +1,4 @@
+import functools
 import jax
 import jax.numpy as jnp
 from jax import lax
@@ -11,6 +12,13 @@
 rope_theta = 500000.0
 stretch_factor = 8.0
 eps = 1e-05
+
+
+def work_the_lines(q_in, named_axis):
+    return jnp.sum(jax.lax.all_gather(q_in, named_axis), axis=0)
+
+
+_try_all_threads = functools.partial(work_the_lines, named_axis="row")
 
 
 def from_behind(value, axis, steps):
@@ -111,8 +119,8 @@
     )
     col_width = out_block.shape[1]
     total_rows = row_count * col_count * slot_count
-    projected = lax.psum(
-        partial_value.reshape(total_rows, col_width).astype(jnp.bfloat16), "row"
+    projected = _try_all_threads(
+        partial_value.reshape(total_rows, col_width).astype(jnp.bfloat16)
     ).astype(jnp.float32)
     stream = residual.astype(jnp.float32) + projected
     squares = lax.psum(jnp.sum(stream * stream, axis=1), "col")

time: 440 us -> 426 us (0.968)
  waiting for transfers between devices: 309 us -> 298 us
  blocking collectives: 63.1 us -> 58.6 us
    psum x1 -> x0, waiting for transfers between devices: 68.6 us -> none  [local(): lax.psum(partial_value.reshape(total_rows, col_width).astype(jnp.bfloat16...]
    all_gather x0 -> x1, waiting for transfers between devices: none -> 54.6 us  [work_the_lines(): return jnp.sum(jax.lax.all_gather(q_in, named_axis), axis=0)]
    psum x1, blocking collectives: 31.7 us -> 27.2 us  [local(): squares = lax.psum(jnp.sum(stream * stream, axis=1), 'col')]
where the time goes in v1:
time: 426 us
  waiting for transfers between devices  298 us (70%)
  blocking collectives  58.6 us (14%)
  local copies, waits for them, and re-layouts  19 us (4%)
  other arithmetic  15.3 us (4%)
  matrix products  14.2 us (3%)
  between operations  13.4 us (3%)
  starting transfers between devices  7.2 us (2%)
    psum x1, waiting for transfers between devices, local(): lax.psum(up_part.astype(jnp.bfloat16), 'col').astype(jnp.float32)  133 us
    psum x1, waiting for transfers between devices, local(): lax.psum(down_part.astype(jnp.bfloat16), 'row').astype(jnp.float32)  70 us
    all_gather x1, waiting for transfers between devices, work_the_lines(): return jnp.sum(jax.lax.all_gather(q_in, named_axis), axis=0)  54.6 us
    all_gather x1, waiting for transfers between devices, local(): lax.all_gather(sectioned, 'col', axis=1, tiled=True)  34.6 us
    psum x1, blocking collectives, local(): squares = lax.psum(jnp.sum(stream * stream, axis=1), 'col')  27.2 us
    all_to_all x1, blocking collectives, local(): lax.all_to_all(mine_rows, 'col', split_axis=0, concat_axis=1, tiled=True)  16.1 us
    all_to_all x1, blocking collectives, local(): lax.all_to_all(moved, 'row', split_axis=1, concat_axis=0, tiled=True)  15.3 us
    unnamed x21, local copies, waits for them, and re-layouts  12.2 us
  transfers between devices with their start and end apart: 6, of which 6 were waited for; matrix products, arithmetic and copies ran while one was open for 0% of the time, Pallas kernels for 0%

profile of v1, /device:TPU:1, one launch (start us, length us, event | category | flops | bytes accessed | tf_op | source)
XLA Modules:
  0.0 425.7 jit_solution(523211680710189439)
XLA Ops:
  6.5 0.8 convert_element_type.84
  7.3 0.7 multiply_add_fusion
  8.0 0.7 iota_compare_fusion
  8.7 3.9 copy.23
  12.7 4.2 fusion.50
  16.8 3.8 copy.32
  20.6 3.8 copy.33
  24.9 1.9 multiply_cosine_fusion
  27.1 4.7 %subtract_convert_fusion = (bf16[4,256,8,64]{3,1,2,0:T(8,128)(2,1)S(1)}, bf16[4,256,8,64]{3,1,2,0:T(8,128)(2,1)S(1)}) fusion(f32[4,256,8,64]{3,1,2,0:T(8,128)} %copy.33, f32[4,256,8,64]{3,1,2,0:T(8,128)} %copy.32, f32[4,256,64]{2,1,0:T(8,128)S(1)} %get-tuple-element.22, f32[4,256,64]{2,1,0:T(8,128)S(1)} %get-tuple-element.21), kind=kLoop, calls=%fused_computation.3 | loop fusion | flops 4194304 | bytes 6815744 | tf_op jit(solution)/shard_map/convert.7
  31.8 1.3 select_reduce_fusion
  33.4 0.6 copy.36
  34.6 5.8 %collective-permute-start = (bf16[4,8,1024]{2,0,1:T(4,128)(2,1)S(1)}, bf16[4,8,1024]{2,0,1:T(4,128)(2,1)S(1)}, u32[]{:S(2)}, u32[]{:S(2)}) collective-permute-start(bf16[4,8,1024]{2,0,1:T(4,128)(2,1)S(1)} %copy.27), channel_id=1, source_target_pairs={{0,128},{1,129},{2,130},{3,131},{4,132},{5,133},{6,134},{7,135},{8... | collective-permute-start | bytes 196616 | tf_op jit(solution)/shard_map/ppermute | solution.py:27
  40.4 1.3 collective-permute-done
  41.7 15.3 %all_to_all.34 = bf16[4,8,1024]{2,0,1:T(4,128)(2,1)S(1)} all-to-all(bf16[4,8,1024]{2,0,1:T(4,128)(2,1)S(1)} %collective-permute-done), channel_id=1, replica_groups=mesh['side'=2,'row'=8,'col'=16] {'row'}, dimensions={1} | all-to-all | bytes 131072 | tf_op jit(solution)/shard_map/all_to_all | solution.py:111
  57.0 0.6 copy.28
  57.7 34.6 %all-gather.5.cloned.1.call-done = bf16[8,64,1,1024]{3,0,2,1:T(8,128)(2,1)} async-done(((bf16[8,4,1,1024]{3,0,2,1:T(8,128)(2,1)}), bf16[8,64,1,1024]{3,0,2,1:T(8,128)(2,1)}) %all-gather.5.cloned.1.call-update) | async-done | bytes 1048592 | tf_op jit(solution)/shard_map/all_gather | solution.py:116
  92.4 1.8 copy.29
  94.2 1.5 convolution_convert_fusion.2
  95.8 54.6 %all-gather.7.cloned.1.call-done = bf16[4096,512]{1,0:T(8,128)(2,1)} async-done(((bf16[512,512]{1,0:T(8,128)(2,1)}), bf16[4096,512]{1,0:T(8,128)(2,1)}) %all-gather.7.cloned.1.call-update) | async-done | bytes 4194320 | tf_op jit(solution)/shard_map/all_gather | solution.py:18
  150.4 3.1 reduce_sum.31
  153.5 1.3 multiply_reduce_fusion
  154.7 27.2 %psum.28 = f32[512]{0:T(512)S(1)} all-reduce(f32[512]{0:T(512)S(1)} %get-tuple-element.13), channel_id=1, replica_groups=mesh['side'=2,'row'=8,'col'=16] {'col'}, use_global_device_ids=true, to_apply=%region_4.5 | all-reduce | flops 512 | bytes 4096 | tf_op jit(solution)/shard_map/psum | solution.py:126
  181.9 3.6 convolution_convert_fusion.1
  185.6 2.5 convolution_convert_fusion
  188.1 132.6 %all-reduce.6.cloned.1.call-done = (bf16[512,1792]{1,0:T(8,128)(2,1)}, bf16[512,1792]{1,0:T(8,128)(2,1)}) async-done(((bf16[512,1792]{1,0:T(8,128)(2,1)}, bf16[512,1792]{1,0:T(8,128)(2,1)}), (bf16[512,1792]{1,0:T(8,128)(2,1)}, bf16[512,1792]{1,0:T(8,128)(2,1)})) %all-reduce.6.cloned.1.call-update) | async-done | bytes 3670032 | tf_op jit(solution)/shard_map/psum | solution.py:138
  320.7 4.6 %fusion.16 = bf16[512,512]{1,0:T(8,128)(2,1)} fusion(bf16[1,1792,512]{2,1,0:T(8,128)(2,1)} %param.21, bf16[512,1792]{1,0:T(8,128)(2,1)} %get-tuple-element.5, bf16[512,1792]{1,0:T(8,128)(2,1)} %get-tuple-element.6), kind=kOutput, calls=%fused_computation.21 | convolution fusion | flops 947126272 | bytes 6029312 | tf_op jit(solution)/shard_map/dot_general | solution.py:141
  325.4 70.0 %all-reduce.4.cloned.1.call-done = bf16[512,512]{1,0:T(8,128)(2,1)} async-done(((bf16[512,512]{1,0:T(8,128)(2,1)}), bf16[512,512]{1,0:T(8,128)(2,1)}) %all-reduce.4.cloned.1.call-update) | async-done | bytes 524304 | tf_op jit(solution)/shard_map/psum | solution.py:142
  395.4 0.9 fusion.37
  396.3 16.1 %all_to_all.35 = bf16[16,4,512]{2,1,0:T(4,128)(2,1)S(1)} all-to-all(bf16[16,4,512]{2,1,0:T(4,128)(2,1)S(1)} %all_to_all.28), channel_id=1, replica_groups=mesh['side'=2,'row'=8,'col'=16] {'col'}, dimensions={0} | all-to-all | bytes 131072 | tf_op jit(solution)/shard_map/all_to_all | solution.py:146
  412.3 1.3 collective-permute-start.1
  413.6 4.9 %collective-permute-done.1 = bf16[4,4096]{1,0:T(4,128)(2,1)S(1)} collective-permute-done((bf16[4,4096]{1,0:T(4,128)(2,1)S(1)}, bf16[4,4096]{1,0:T(4,128)(2,1)S(1)}, u32[]{:S(2)}, u32[]{:S(2)}) %collective-permute-start.1) | collective-permute-done | bytes 32800 | tf_op jit(solution)/shard_map/ppermute | solution.py:27
  418.5 0.6 slice_select_fusion
  (45 shorter events, 1.7 us)
Async XLA Ops:
  6.5 175.4 %copy-start = (bf16[1,512,1792]{2,1,0:T(8,128)(2,1)S(1)}, bf16[1,512,1792]{2,1,0:T(8,128)(2,1)}, u32[]{:S(2)}) copy-start(bf16[1,512,1792]{2,1,0:T(8,128)(2,1)} %param.19) | copy-start | bytes 5505028
  6.5 85.8 %all-gather.5.cloned.1.call-start = ((), (), s32[]{:S(2)}) async-start(), calls=%async_computation.3 | async-start | bytes 1114112 | tf_op jit(solution)/shard_map/all_gather | solution.py:116
  20.6 3.8 copy-start.3
  20.6 3.9 copy-start.4
  31.8 1.6 copy-start.1
  34.5 59.7 %copy-start.7 = (bf16[1,1024,512]{2,1,0:T(8,128)(2,1)S(1)}, bf16[1,1024,512]{2,1,0:T(8,128)(2,1)}, u32[]{:S(2)}) copy-start(bf16[1,1024,512]{2,1,0:T(8,128)(2,1)} %param.18) | copy-start | bytes 3145732
  34.6 7.1 %collective-permute-start = (bf16[4,8,1024]{2,0,1:T(4,128)(2,1)S(1)}, bf16[4,8,1024]{2,0,1:T(4,128)(2,1)S(1)}, u32[]{:S(2)}, u32[]{:S(2)}) collective-permute-start(bf16[4,8,1024]{2,0,1:T(4,128)(2,1)S(1)} %copy.27), channel_id=1, source_target_pairs={{0,128},{1,129},{2,130},{3,131},{4,132},{5,133},{6,134},{7,135},{8... | collective-permute-start | bytes 196616 | tf_op jit(solution)/shard_map/ppermute | solution.py:27
  57.7 92.7 %all-gather.7.cloned.1.call-start = ((), (), s32[]{:S(2)}) async-start(), calls=%async_computation.4 | async-start | bytes 4718592 | tf_op jit(solution)/shard_map/all_gather | solution.py:18
  94.2 1.6 copy-start.5
  95.7 225.0 %all-reduce.6.cloned.1.call-start = ((), (), s32[]{:S(2)}) async-start(), calls=%async_computation.5 | async-start | bytes 7340032 | tf_op jit(solution)/shard_map/psum | solution.py:138
  181.9 3.7 copy-start.2
  181.9 3.7 copy-start.6
  188.1 207.3 %all-reduce.4.cloned.1.call-start = ((), (), s32[]{:S(2)}) async-start(), calls=%async_computation.2 | async-start | bytes 1048576 | tf_op jit(solution)/shard_map/psum | solution.py:142
  412.3 6.2 %collective-permute-start.1 = (bf16[4,4096]{1,0:T(4,128)(2,1)S(1)}, bf16[4,4096]{1,0:T(4,128)(2,1)S(1)}, u32[]{:S(2)}, u32[]{:S(2)}) collective-permute-start(bf16[4,4096]{1,0:T(4,128)(2,1)S(1)} %slice.46), channel_id=1, source_target_pairs={{128,0},{129,1},{130,2},{131,3},{132,4},{133,5},{134,6},{135,7},{1... | collective-permute-start | bytes 98312 | tf_op jit(solution)/shard_map/ppermute | solution.py:27
Sparse Core Ops, SparseCore 0:
  57.8 34.5 all-gather.4
  95.8 54.5 all-gather.6
  188.2 132.4 all-reduce.5
  325.5 69.8 all-reduce.3
